TPU v7x, 256 devices: a whole 4x4x8 slice. The times are simulated.
256 devices in a mesh: dp: 2 (over core), row: 16 (over y, x), col: 8 (over z).
Axes of the slice: x: 4, y: 4, z: 8, core: 2. Of those that a mesh axis runs over, the one named last changes fastest.
Arguments:
- features: bfloat16 [256, 96, 2048], P(('dp', 'row'), 'col'), parts along dimension 0, may hold values from 0 to 40
- low_level: bfloat16 [512, 192, 256], P(('dp', 'row'), 'col'), parts along dimension 0, may hold values from -6 to 6
- point_weight: bfloat16 [2048, 256], P(None, 'row'), may hold values from -0.125 to 0.125
- atrous_weight: bfloat16 [3, 3, 3, 2048, 256], P(None, None, None, None, 'row'), may hold values from -0.046875 to 0.046875
- pool_weight: bfloat16 [2048, 256], P(None, 'row'), may hold values from -0.125 to 0.125
- aspp_bias: float32 [5, 256], P(None, 'row'), may hold values from -1.5 to 1.5
- proj_weight: bfloat16 [1280, 256], replicated, may hold values from -0.15625 to 0.15625
- proj_bias: float32 [256], replicated, may hold values from -1.5 to 1.5
- low_weight: bfloat16 [256, 48], replicated, may hold values from -0.375 to 0.375
- low_bias: float32 [48], replicated, may hold values from -1.5 to 1.5
- conv1_weight: bfloat16 [3, 3, 304, 256], replicated, may hold values from -0.109375 to 0.109375
- conv1_bias: float32 [256], replicated, may hold values from -1.5 to 1.5
- conv2_weight: bfloat16 [3, 3, 256, 256], replicated, may hold values from -0.125 to 0.125
- conv2_bias: float32 [256], replicated, may hold values from -1.5 to 1.5
Outputs:
- decoded: bfloat16 [512, 192, 256], P(('dp', 'row'), 'col'), parts along dimension 0
There are 2 independent parts, one for each index of `dp`. A program takes and returns all parts, laid end to end along the dimension named above; an argument that names none is the same for every part. Nothing has to cross between parts.
All inputs are finite; a program needn't handle non-finite values.
Results may differ from a plain program's by a relative error of at most 0.0057.
Values may be sent and summed in bfloat16 or wider, within the bound.
No kernel may reach another device: no remote copies, remote signals or barrier semaphores. Data moves between devices by JAX's collectives and lax.ppermute only.
A program may use at most 128 MiB of HBM per device.

v0:
```python
import jax
import jax.numpy as jnp
from jax import lax
from jax.sharding import Mesh
from jax.sharding import PartitionSpec as P

ROW = ("row_0", "row_1")
ROW_COL = ("row_0", "row_1", "col")
DP_ROW = ("dp", "row_0", "row_1")
RATES = (12, 24, 36)


def from_behind(value, axis, by):
    devices = lax.axis_size(axis)
    pairs = [(i, i + by) for i in range(devices) if 0 <= i + by < devices]
    return lax.ppermute(value, axis, pairs)


def one_axis_at_a_time(value, axes):
    for axis in axes:
        value = lax.psum(value, axis)
    return value


def padded_2(value, sides, width):
    for axis, dim in sides:
        devices, length = (lax.axis_size(axis), value.shape[dim])
        up = [(i, (i + 1) % devices) for i in range(devices - 1)]
        down = [(j, i) for i, j in up]
        last = lax.slice_in_dim(value, length - width, length, axis=dim)
        first = lax.slice_in_dim(value, 0, width, axis=dim)
        before = lax.ppermute(last, axis, up)
        after = lax.ppermute(first, axis, down)
        value = jnp.concatenate([before, value, after], axis=dim)
    return value


def enlarge(padded):
    values = padded.astype(jnp.float32)
    middle = values[1:-1]
    even = 0.75 * middle + 0.25 * values[:-2]
    odd = 0.75 * middle + 0.25 * values[2:]
    values = jnp.stack([even, odd], axis=1).reshape(
        2 * middle.shape[0], middle.shape[1], middle.shape[2]
    )
    middle = values[:, 1:-1]
    even = 0.75 * middle + 0.25 * values[:, :-2]
    odd = 0.75 * middle + 0.25 * values[:, 2:]
    values = jnp.stack([even, odd], axis=2).reshape(
        values.shape[0], 2 * middle.shape[1], middle.shape[2]
    )
    return values.astype(jnp.bfloat16)


def convolve(padded, weight, bias):
    height, width = (padded.shape[0] - 2, padded.shape[1] - 2)
    windows = []
    for row_tap in range(3):
        for col_tap in range(3):
            windows.append(padded[row_tap : row_tap + height, col_tap : col_tap + width])
    columns = jnp.concatenate(windows, axis=2)
    depth = columns.shape[2]
    result = jnp.dot(
        columns.reshape(-1, depth), weight.reshape(depth, -1), preferred_element_type=jnp.float32
    )
    result = jnp.maximum(result + bias, 0.0).astype(jnp.bfloat16)
    return result.reshape(height, width, -1)


def local_rows(values, offset):
    height = values.shape[0]
    extent = abs(offset)
    padded = jnp.pad(values, ((extent, extent), (0, 0), (0, 0)))
    return padded[extent + offset : extent + offset + height]


def bring_cols(values, steps):
    if steps == 0:
        return values
    return from_behind(values, "col", steps)


def move_cols(values, distance):
    width = values.shape[1]
    whole = distance // width
    pieces = bring_cols(values, -whole)
    return pieces


def fix_edges(padded, at_start, at_end, axis_number):
    size = padded.shape[axis_number]
    first = lax.slice_in_dim(padded, 0, 1, axis=axis_number)
    second = lax.slice_in_dim(padded, 1, 2, axis=axis_number)
    middle = lax.slice_in_dim(padded, 1, size - 1, axis=axis_number)
    before = lax.slice_in_dim(padded, size - 2, size - 1, axis=axis_number)
    final = lax.slice_in_dim(padded, size - 1, size, axis=axis_number)
    first = jnp.where(at_start, second, first)
    final = jnp.where(at_end, before, final)
    return jnp.concatenate([first, middle, final], axis=axis_number)


def on_device(
    features,
    low_level,
    point_weight,
    atrous_weight,
    pool_weight,
    aspp_bias,
    proj_weight,
    proj_bias,
    low_weight,
    low_bias,
    conv1_weight,
    conv1_bias,
    conv2_weight,
    conv2_bias,
):
    in_width = features.shape[2]
    own_width = point_weight.shape[1]
    out_width = proj_weight.shape[1]
    row_count = lax.axis_size(ROW)
    col_count = lax.axis_size("col")
    row_index = lax.axis_index(ROW)
    col_index = lax.axis_index("col")
    tile_rows, tile_cols = (features.shape[0], features.shape[1])
    full_rows = tile_rows * row_count
    full_cols = tile_cols * col_count
    atrous_flat = jnp.transpose(atrous_weight.reshape(27, in_width, own_width), (1, 0, 2)).reshape(
        in_width, 27 * own_width
    )
    own_stack = jnp.concatenate([point_weight, atrous_flat, pool_weight], axis=1)
    group_total = 28
    stacked = own_stack[:, : group_total * own_width]
    piece = lax.all_gather(features, ROW, axis=0, tiled=True)
    result = jnp.dot(piece.reshape(-1, in_width), stacked, preferred_element_type=jnp.float32)
    products = result.reshape(piece.shape[0], piece.shape[1], -1)
    map_rows = products.shape[0]

    def group(number):
        return products[:, :, number * own_width : (number + 1) * own_width]

    all_width = own_width * row_count
    first_col = jnp.where(col_index == 0, 1.0, 0.0).astype(jnp.float32)
    spread_bias = lax.dynamic_update_slice_in_dim(
        jnp.zeros((5, all_width), jnp.float32), aspp_bias * first_col, row_index * own_width, 1
    )
    tile_sum = jnp.sum(features.astype(jnp.float32), axis=(0, 1))
    scene_sum, full_bias = (
        one_axis_at_a_time(tile_sum, ROW_COL),
        one_axis_at_a_time(spread_bias, ROW_COL),
    )
    pooled = jnp.dot(
        scene_sum, pool_weight.astype(jnp.float32), precision=lax.Precision.HIGHEST
    ) / (full_rows * full_cols)
    last_axis = full_bias.ndim - 1
    bias_mine = lax.dynamic_slice_in_dim(full_bias, row_index * own_width, own_width, last_axis)

    def activate(values, number):
        return jnp.maximum(values + bias_mine[number], 0.0).astype(jnp.bfloat16)

    outputs = [activate(group(0), 0)]
    for rate_number in range(3):
        dilation = RATES[rate_number]
        running = jnp.zeros((map_rows, tile_cols, own_width), jnp.float32)
        for col_tap in range(3):
            column_sum = jnp.zeros((map_rows, tile_cols, own_width), jnp.float32)
            for row_tap in range(3):
                row_values = group(1 + rate_number * 9 + row_tap * 3 + col_tap)
                offset = (row_tap - 1) * RATES[rate_number]
                column_sum = column_sum + local_rows(row_values, offset)
            running = running + move_cols(column_sum, (col_tap - 1) * dilation)
        outputs.append(activate(running, rate_number + 1))
    pool_branch = jnp.maximum(pooled + bias_mine[4], 0.0).astype(jnp.bfloat16)
    outputs.append(jnp.broadcast_to(pool_branch, (map_rows, tile_cols, own_width)))
    branches = jnp.concatenate(outputs, axis=2)
    blocks = proj_weight.reshape(5, row_count, own_width, out_width)
    swapped = lax.all_to_all(branches, ROW, split_axis=0, concat_axis=2, tiled=True)
    reordered = jnp.transpose(blocks, (1, 0, 2, 3)).reshape(-1, out_width)
    summed = jnp.dot(
        swapped.reshape(-1, swapped.shape[2]), reordered, preferred_element_type=jnp.float32
    )
    coarse = (
        jnp.maximum(summed + proj_bias, 0.0)
        .astype(jnp.bfloat16)
        .reshape(tile_rows, tile_cols, out_width)
    )
    padded = padded_2(coarse, ((ROW, 0), ("col", 1)), 1)
    padded = fix_edges(padded, row_index == 0, row_index == row_count - 1, 0)
    padded = fix_edges(padded, col_index == 0, col_index == col_count - 1, 1)
    upsampled = enlarge(padded)
    low_rows = low_level.reshape(-1, low_level.shape[2])
    reduced = jnp.dot(low_rows, low_weight, preferred_element_type=jnp.float32)
    reduced = (
        jnp.maximum(reduced + low_bias, 0.0)
        .astype(jnp.bfloat16)
        .reshape(low_level.shape[0], low_level.shape[1], -1)
    )
    joined_fine = jnp.concatenate([upsampled, reduced], axis=2)
    padded_fine = padded_2(joined_fine, ((ROW, 0), ("col", 1)), 1)
    hidden = convolve(padded_fine, conv1_weight, conv1_bias)
    padded_hidden = padded_2(hidden, ((ROW, 0), ("col", 1)), 1)
    return convolve(padded_hidden, conv2_weight, conv2_bias)


def solution(mesh):
    torus = Mesh(
        mesh.devices.reshape(mesh.shape["dp"], 4, 4, mesh.shape["col"]),
        ("dp", "row_0", "row_1", "col"),
    )
    placed = (
        P(DP_ROW, "col", None),
        P(DP_ROW, "col", None),
        P(None, ROW),
        P(None, None, None, None, ROW),
        P(None, ROW),
        P(None, ROW),
        P(),
        P(),
        P(),
        P(),
        P(),
        P(),
        P(),
        P(),
    )
    return jax.shard_map(
        on_device, mesh=torus, in_specs=placed, out_specs=P(DP_ROW, "col", None), check_vma=False
    )
```

profile of v0, /device:TPU:70, one launch (start us, length us, event | category | flops | bytes accessed | tf_op | source)
XLA Modules:
  0.0 292.7 jit_solution(2077303134434737102)
XLA Ops:
  9.2 17.2 %all-reduce.20 = (f32[5,256]{1,0:T(8,128)S(1)}, f32[2048]{0:T(1024)S(1)}) all-reduce(f32[5,256]{1,0:T(8,128)S(1)} %dynamic_update_slice.3, f32[2048]{0:T(1024)S(1)} %convert_reduce_fusion), channel_id=1, replica_groups=mesh['dp'=2,'row_0'=4,'row_1'=4,'col'=8] {'row_0'}, use_global_device_ids=true, to_apply=%region_0.1 | all-reduce | flops 3328 | bytes 26624 | tf_op jit(solution)/shard_map/psum | solution.py:21
  26.4 13.9 %all-reduce.19 = (f32[5,256]{1,0:T(8,128)S(1)}, f32[2048]{0:T(1024)S(1)}) all-reduce(f32[5,256]{1,0:T(8,128)S(1)} %get-tuple-element.9, f32[2048]{0:T(1024)S(1)} %get-tuple-element.10), channel_id=1, replica_groups=mesh['dp'=2,'row_0'=4,'row_1'=4,'col'=8] {'row_1'}, use_global_device_ids=true, to_apply=%region_1.2 | all-reduce | flops 3328 | bytes 26624 | tf_op jit(solution)/shard_map/psum | solution.py:21
  40.3 29.7 %all-reduce.18 = (f32[5,256]{1,0:T(8,128)S(1)}, f32[2048]{0:T(1024)S(1)}) all-reduce(f32[5,256]{1,0:T(8,128)S(1)} %get-tuple-element.7, f32[2048]{0:T(1024)S(1)} %get-tuple-element.8), channel_id=1, replica_groups=mesh['dp'=2,'row_0'=4,'row_1'=4,'col'=8] {'col'}, use_global_device_ids=true, to_apply=%region_2.3 | all-reduce | flops 3328 | bytes 26624 | tf_op jit(solution)/shard_map/psum | solution.py:21
  71.0 7.2 %all-gather.2.cloned.1.call-done = bf16[128,12,2048]{2,0,1:T(8,128)(2,1)} async-done(((bf16[8,12,2048]{2,0,1:T(8,128)(2,1)}), bf16[128,12,2048]{2,0,1:T(8,128)(2,1)}) %all-gather.2.cloned.1.call-update) | async-done | bytes 6291472 | tf_op jit(solution)/shard_map/all_gather | solution.py:134
  78.3 9.7 %copy.180 = bf16[128,12,2048]{2,1,0:T(8,128)(2,1)} copy(bf16[128,12,2048]{2,0,1:T(8,128)(2,1)} %all-gather.2.cloned.1.call-done) | data formatting | bytes 12582912 | tf_op jit(solution)/shard_map/all_gather | solution.py:134
  88.0 10.8 %reshape.87 = bf16[1536,2048]{1,0:T(8,128)(2,1)} reshape(bf16[128,12,2048]{2,1,0:T(8,128)(2,1)} %copy.180) | data formatting | bytes 12582912 | tf_op jit(solution)/shard_map/reshape | solution.py:135
  98.9 7.3 %convolution_bitcast_fusion = f32[1536,448]{0,1:T(8,128)} fusion(bf16[1536,2048]{1,0:T(8,128)(2,1)} %reshape.87, bf16[2048,432]{0,1:T(8,128)(2,1)S(1)} %bitcast.118, bf16[2048,16]{0,1:T(8,128)(2,1)S(1)} %copy-done.19), kind=kOutput, calls=%fused_computation | convolution fusion | flops 2822242304 | bytes 10878976 | tf_op jit(solution)/shard_map/dot_general | solution.py:135
  106.2 3.4 %copy.181 = f32[1536,448]{1,0:T(8,128)} copy(f32[1536,448]{0,1:T(8,128)} %convolution_bitcast_fusion) | data formatting | bytes 5505024 | tf_op jit(solution)/shard_map/dot_general | solution.py:135
  109.6 4.6 %reshape.88 = f32[128,12,448]{2,1,0:T(8,128)} reshape(f32[1536,448]{1,0:T(8,128)} %copy.181) | data formatting | bytes 5505024 | tf_op jit(solution)/shard_map/reshape | solution.py:136
  114.2 13.5 %fusion.61 = (f32[128,12,16]{2,1,0:T(8,128)}, f32[128,12,16]{2,1,0:T(8,128)}, f32[128,12,16]{2,1,0:T(8,128)}, f32[128,12,16]{2,1,0:T(8,128)}, f32[128,12,16]{2,1...) fusion(f32[128,12,448]{2,1,0:T(8,128)} %reshape.88), kind=kLoop, calls=%fused_computation.144 | loop fusion | bytes 3735552 | tf_op jit(solution)/shard_map/slice | solution.py:140
  127.7 2.2 copy.224
  129.9 2.2 copy.225
  132.0 2.2 copy.223
  134.2 2.2 copy.222
  136.3 2.2 copy.221
  138.5 2.2 copy.220
  140.7 2.2 copy.219
  145.1 8.7 %fusion.62 = (f32[128,12,16]{2,1,0:T(8,128)}, f32[128,12,16]{2,1,0:T(8,128)}, f32[128,12,16]{2,1,0:T(8,128)}, f32[128,12,16]{2,1,0:T(8,128)}, f32[128,12,16]{2,1...) fusion(f32[128,12,448]{2,1,0:T(8,128)} %reshape.88, ...), kind=kLoop, calls=%fused_computation.145 | loop fusion | flops 245760 | bytes 2555904 | tf_op jit(solution)/shard_map/slice | solution.py:140
  158.6 2.3 copy.188
  160.9 2.1 copy.187
  165.4 2.4 collective-permute-start.1
  167.8 6.6 %collective-permute-start.2 = (f32[128,12,16]{0,2,1:T(8,128)}, f32[128,12,16]{0,2,1:T(8,128)}, u32[]{:S(2)}, u32[]{:S(2)}) collective-permute-start(f32[128,12,16]{0,2,1:T(8,128)} %copy.188), channel_id=1, source_target_pairs={{0,2},{1,3},{2,4},{3,5},{4,6},{5,7},{8,10},{9,11},{10,12},{11,13},... | collective-permute-start | bytes 294920 | tf_op jit(solution)/shard_map/ppermute | solution.py:16
  174.4 6.7 %collective-permute-start.4 = (f32[128,12,16]{0,2,1:T(8,128)}, f32[128,12,16]{0,2,1:T(8,128)}, u32[]{:S(2)}, u32[]{:S(2)}) collective-permute-start(f32[128,12,16]{0,2,1:T(8,128)} %copy.193), channel_id=1, source_target_pairs={{0,3},{1,4},{2,5},{3,6},{4,7},{8,11},{9,12},{10,13},{11,14},{12,15... | collective-permute-start | bytes 294920 | tf_op jit(solution)/shard_map/ppermute | solution.py:16
  181.1 1.9 collective-permute-start
  185.6 3.8 %collective-permute-start.3 = (f32[128,12,16]{0,2,1:T(8,128)}, f32[128,12,16]{0,2,1:T(8,128)S(1)}, u32[]{:S(2)}, u32[]{:S(2)}) collective-permute-start(f32[128,12,16]{0,2,1:T(8,128)} %copy.192), channel_id=1, source_target_pairs={{2,0},{3,1},{4,2},{5,3},{6,4},{7,5},{10,8},{11,9},{12,10},{13,11},... | collective-permute-start | bytes 294920 | tf_op jit(solution)/shard_map/ppermute | solution.py:16
  190.0 1.9 fusion.59
  192.0 2.7 collective-permute-done.3
  201.7 5.7 %all-to-all-start = ((bf16[16,2,3840]{2,1,0:T(2,128)(2,1)}), bf16[16,2,3840]{2,1,0:T(2,128)(2,1)S(1)}, u32[]{:S(2)}, u32[]{:S(2)}) async-start(bf16[16,2,3840]{2,1,0:T(2,128)(2,1)} %reshape.102), calls=%async_computation | async-start | bytes 491520 | tf_op jit(solution)/shard_map/all_to_all | solution.py:177
  207.5 6.2 %all-to-all-done = bf16[16,2,3840]{2,1,0:T(2,128)(2,1)S(1)} async-done(((bf16[16,2,3840]{2,1,0:T(2,128)(2,1)}), bf16[16,2,3840]{2,1,0:T(2,128)(2,1)S(1)}, u32[]{:S(2)}, u32[]{:S(2)}) %all-to-all-start) | async-done | bytes 245792 | tf_op jit(solution)/shard_map/all_to_all | solution.py:177
  215.4 3.6 %collective-permute-start.6 = (bf16[1,12,256]{2,1,0:T(8,128)(2,1)S(1)}, bf16[1,12,256]{2,1,0:T(8,128)(2,1)S(1)}, u32[]{:S(2)}, u32[]{:S(2)}) collective-permute-start(bf16[1,12,256]{2,1,0:T(8,128)(2,1)S(1)} %get-tuple-element.77), channel_id=1, source_target_pairs={{0,8},{8,16},{16,24},{24,32},{32,40},{40,48},{48,56},{56,64},{64,7... | collective-permute-start | bytes 18440 | tf_op jit(solution)/shard_map/ppermute | solution.py:32
  219.1 2.2 collective-permute-start.7
  221.4 5.4 %collective-permute-done.7 = bf16[1,12,256]{2,1,0:T(8,128)(2,1)S(1)} collective-permute-done((bf16[1,12,256]{2,1,0:T(8,128)(2,1)S(1)}, bf16[1,12,256]{2,1,0:T(8,128)(2,1)S(1)}, u32[]{:S(2)}, u32[]{:S(2)}) %collective-permute-start.7) | collective-permute-done | bytes 6176 | tf_op jit(solution)/shard_map/ppermute | solution.py:33
  226.8 1.9 collective-permute-start.8
  228.7 3.9 %collective-permute-start.9 = (bf16[10,1,256]{2,1,0:T(2,128)(2,1)S(1)}, bf16[10,1,256]{2,1,0:T(2,128)(2,1)S(1)}, u32[]{:S(2)}, u32[]{:S(2)}) collective-permute-start(bf16[10,1,256]{2,1,0:T(2,128)(2,1)S(1)} %get-tuple-element.75), channel_id=1, source_target_pairs={{1,0},{2,1},{3,2},{4,3},{5,4},{6,5},{7,6},{9,8},{10,9},{11,10},{12... | collective-permute-start | bytes 15368 | tf_op jit(solution)/shard_map/ppermute | solution.py:33
  235.1 1.9 collective-permute-start.10
  237.1 3.9 %collective-permute-start.11 = (bf16[1,24,304]{2,0,1:T(2,128)(2,1)S(1)}, bf16[1,24,304]{2,0,1:T(2,128)(2,1)S(1)}, u32[]{:S(2)}, u32[]{:S(2)}) collective-permute-start(bf16[1,24,304]{2,0,1:T(2,128)(2,1)S(1)} %get-tuple-element.57), channel_id=1, source_target_pairs={{8,0},{16,8},{24,16},{32,24},{40,32},{48,40},{56,48},{64,56},{72,6... | collective-permute-start | bytes 43784 | tf_op jit(solution)/shard_map/ppermute | solution.py:33
  242.0 3.1 %collective-permute-done.11 = bf16[1,24,304]{2,0,1:T(2,128)(2,1)S(1)} collective-permute-done((bf16[1,24,304]{2,0,1:T(2,128)(2,1)S(1)}, bf16[1,24,304]{2,0,1:T(2,128)(2,1)S(1)}, u32[]{:S(2)}, u32[]{:S(2)}) %collective-permute-start.11) | collective-permute-done | bytes 14624 | tf_op jit(solution)/shard_map/ppermute | solution.py:33
  245.1 4.1 %collective-permute-start.13 = (bf16[18,1,304]{2,0,1:T(8,128)(2,1)S(1)}, bf16[18,1,304]{2,0,1:T(8,128)(2,1)S(1)}, u32[]{:S(2)}, u32[]{:S(2)}) collective-permute-start(bf16[18,1,304]{2,0,1:T(8,128)(2,1)S(1)} %get-tuple-element.46), channel_id=1, source_target_pairs={{1,0},{2,1},{3,2},{4,3},{5,4},{6,5},{7,6},{9,8},{10,9},{11,10},{12... | collective-permute-start | bytes 32840 | tf_op jit(solution)/shard_map/ppermute | solution.py:33
  249.2 1.9 collective-permute-start.12
  251.6 3.3 %collective-permute-done.12 = bf16[18,1,304]{2,0,1:T(8,128)(2,1)S(1)} collective-permute-done((bf16[18,1,304]{2,0,1:T(8,128)(2,1)S(1)}, bf16[18,1,304]{2,0,1:T(8,128)(2,1)S(1)}, u32[]{:S(2)}, u32[]{:S(2)}) %collective-permute-start.12) | collective-permute-done | bytes 10976 | tf_op jit(solution)/shard_map/ppermute | solution.py:32
  256.8 4.9 %concatenate.122 = bf16[384,2736]{1,0:T(8,128)(2,1)} concatenate(bf16[384,304]{1,0:T(8,128)(2,1)S(1)} %bitcast.104, bf16[384,304]{1,0:T(8,128)(2,1)S(1)} %bitcast.100, bf16[384,304]{1,0:T(8,128)(2,1)S(1)} %bitcast.103, bf16[384,304]{1,0:T(8,128)(2,1)S(1)} %bitcast.105, bf16[384,256]{1,0:T(8,128)(2,1)} %convert_element_type.76, bf16[384,48]{1,0:T(8,128)(2,1)} %copy-done.6, ...), dimensions={1} | concatenate | bytes 4202496 | tf_op jit(solution)/shard_map/concatenate | solution.py:61
  261.7 2.3 fusion.6
  264.1 1.9 collective-permute-start.14
  266.0 3.9 %collective-permute-start.15 = (bf16[1,24,256]{2,1,0:T(8,128)(2,1)S(1)}, bf16[1,24,256]{2,1,0:T(8,128)(2,1)S(1)}, u32[]{:S(2)}, u32[]{:S(2)}) collective-permute-start(bf16[1,24,256]{2,1,0:T(8,128)(2,1)S(1)} %get-tuple-element.67), channel_id=1, source_target_pairs={{8,0},{16,8},{24,16},{32,24},{40,32},{48,40},{56,48},{64,56},{72,6... | collective-permute-start | bytes 36872 | tf_op jit(solution)/shard_map/ppermute | solution.py:33
  269.9 3.8 %collective-permute-done.15 = bf16[1,24,256]{2,1,0:T(8,128)(2,1)S(1)} collective-permute-done((bf16[1,24,256]{2,1,0:T(8,128)(2,1)S(1)}, bf16[1,24,256]{2,1,0:T(8,128)(2,1)S(1)}, u32[]{:S(2)}, u32[]{:S(2)}) %collective-permute-start.15) | collective-permute-done | bytes 12320 | tf_op jit(solution)/shard_map/ppermute | solution.py:33
  273.7 3.5 %collective-permute-start.17 = (bf16[18,1,256]{2,1,0:T(2,128)(2,1)S(1)}, bf16[18,1,256]{2,1,0:T(2,128)(2,1)S(1)}, u32[]{:S(2)}, u32[]{:S(2)}) collective-permute-start(bf16[18,1,256]{2,1,0:T(2,128)(2,1)S(1)} %get-tuple-element.62), channel_id=1, source_target_pairs={{1,0},{2,1},{3,2},{4,3},{5,4},{6,5},{7,6},{9,8},{10,9},{11,10},{12... | collective-permute-start | bytes 27656 | tf_op jit(solution)/shard_map/ppermute | solution.py:33
  277.3 2.3 collective-permute-start.16
  279.6 3.3 %collective-permute-done.16 = bf16[18,1,256]{2,1,0:T(2,128)(2,1)S(1)} collective-permute-done((bf16[18,1,256]{2,1,0:T(2,128)(2,1)S(1)}, bf16[18,1,256]{2,1,0:T(2,128)(2,1)S(1)}, u32[]{:S(2)}, u32[]{:S(2)}) %collective-permute-start.16) | collective-permute-done | bytes 9248 | tf_op jit(solution)/shard_map/ppermute | solution.py:32
  (139 shorter events, 33.7 us)
Async XLA Ops:
  6.5 255.2 %copy-start = (bf16[3,3,304,256]{3,2,1,0:T(8,128)(2,1)S(1)}, bf16[3,3,304,256]{3,2,1,0:T(8,128)(2,1)}, u32[]{:S(2)}) copy-start(bf16[3,3,304,256]{3,2,1,0:T(8,128)(2,1)} %param.24) | copy-start | bytes 4202500
  6.5 71.7 %all-gather.2.cloned.1.call-start = ((), (), s32[]{:S(2)}) async-start(), calls=%async_computation.1 | async-start | bytes 6684672 | tf_op jit(solution)/shard_map/all_gather | solution.py:134
  88.0 10.8 %copy-start.17 = (bf16[3,3,3,2048,16]{3,4,2,1,0:T(8,128)(2,1)S(1)}, bf16[3,3,3,2048,16]{3,4,2,1,0:T(8,128)(2,1)}, u32[]{:S(2)}) copy-start(bf16[3,3,3,2048,16]{3,4,2,1,0:T(8,128)(2,1)} %param.17) | copy-start | bytes 5308420
  88.0 10.8 %copy-start.19 = (bf16[2048,16]{0,1:T(8,128)(2,1)S(1)}, bf16[2048,16]{0,1:T(8,128)(2,1)}, u32[]{:S(2)}) copy-start(bf16[2048,16]{0,1:T(8,128)(2,1)} %param.16) | copy-start | bytes 196612
  143.8 1.2 copy-start.1
  153.8 2.7 copy-start.5
  156.4 1.2 copy-start.4
  157.4 5.6 %copy-start.3 = (f32[128,12,16]{2,1,0:T(8,128)S(1)}, f32[128,12,16]{2,1,0:T(8,128)}, u32[]{:S(2)}) copy-start(f32[128,12,16]{2,1,0:T(8,128)} %get-tuple-element.35) | copy-start | bytes 294916
  158.6 26.0 %copy-start.2 = (f32[128,12,16]{2,1,0:T(8,128)S(1)}, f32[128,12,16]{2,1,0:T(8,128)}, u32[]{:S(2)}) copy-start(f32[128,12,16]{2,1,0:T(8,128)} %get-tuple-element.31) | copy-start | bytes 294916
  164.0 30.6 %copy-start.10 = (f32[128,12,16]{0,2,1:T(8,128)S(1)}, f32[128,12,16]{0,2,1:T(8,128)}, u32[]{:S(2)}) copy-start(f32[128,12,16]{0,2,1:T(8,128)} %copy.223) | copy-start | bytes 294916
  164.0 32.4 %copy-start.8 = (f32[128,12,16]{0,2,1:T(8,128)S(1)}, f32[128,12,16]{0,2,1:T(8,128)}, u32[]{:S(2)}) copy-start(f32[128,12,16]{0,2,1:T(8,128)} %copy.224) | copy-start | bytes 294916
  164.0 32.4 %copy-start.9 = (f32[128,12,16]{0,2,1:T(8,128)S(1)}, f32[128,12,16]{0,2,1:T(8,128)}, u32[]{:S(2)}) copy-start(f32[128,12,16]{0,2,1:T(8,128)} %copy.225) | copy-start | bytes 294916
  164.0 32.4 %collective-permute-start.5 = (f32[128,12,16]{0,2,1:T(8,128)}, f32[128,12,16]{0,2,1:T(8,128)}, u32[]{:S(2)}, u32[]{:S(2)}) collective-permute-start(f32[128,12,16]{0,2,1:T(8,128)} %copy.197), channel_id=1, source_target_pairs={{3,0},{4,1},{5,2},{6,3},{7,4},{11,8},{12,9},{13,10},{14,11},{15,12... | collective-permute-start | bytes 294920 | tf_op jit(solution)/shard_map/ppermute | solution.py:16
  165.4 20.1 %collective-permute-start.1 = (f32[128,12,16]{0,2,1:T(8,128)}, f32[128,12,16]{0,2,1:T(8,128)S(1)}, u32[]{:S(2)}, u32[]{:S(2)}) collective-permute-start(f32[128,12,16]{0,2,1:T(8,128)} %copy.187), channel_id=1, source_target_pairs={{1,0},{2,1},{3,2},{4,3},{5,4},{6,5},{7,6},{9,8},{10,9},{11,10},{12... | collective-permute-start | bytes 294920 | tf_op jit(solution)/shard_map/ppermute | solution.py:16
  167.8 24.2 %collective-permute-start.2 = (f32[128,12,16]{0,2,1:T(8,128)}, f32[128,12,16]{0,2,1:T(8,128)}, u32[]{:S(2)}, u32[]{:S(2)}) collective-permute-start(f32[128,12,16]{0,2,1:T(8,128)} %copy.188), channel_id=1, source_target_pairs={{0,2},{1,3},{2,4},{3,5},{4,6},{5,7},{8,10},{9,11},{10,12},{11,13},... | collective-permute-start | bytes 294920 | tf_op jit(solution)/shard_map/ppermute | solution.py:16
  174.4 22.0 %collective-permute-start.4 = (f32[128,12,16]{0,2,1:T(8,128)}, f32[128,12,16]{0,2,1:T(8,128)}, u32[]{:S(2)}, u32[]{:S(2)}) collective-permute-start(f32[128,12,16]{0,2,1:T(8,128)} %copy.193), channel_id=1, source_target_pairs={{0,3},{1,4},{2,5},{3,6},{4,7},{8,11},{9,12},{10,13},{11,14},{12,15... | collective-permute-start | bytes 294920 | tf_op jit(solution)/shard_map/ppermute | solution.py:16
  181.1 8.3 %collective-permute-start = (f32[128,12,16]{0,2,1:T(8,128)}, f32[128,12,16]{0,2,1:T(8,128)S(1)}, u32[]{:S(2)}, u32[]{:S(2)}) collective-permute-start(f32[128,12,16]{0,2,1:T(8,128)} %copy.183), channel_id=1, source_target_pairs={{0,1},{1,2},{2,3},{3,4},{4,5},{5,6},{6,7},{8,9},{9,10},{10,11},{11... | collective-permute-start | bytes 294920 | tf_op jit(solution)/shard_map/ppermute | solution.py:16
  185.6 3.8 %copy-start.12 = (f32[128,12,16]{0,2,1:T(8,128)}, f32[128,12,16]{0,2,1:T(8,128)S(1)}, u32[]{:S(2)}) copy-start(f32[128,12,16]{0,2,1:T(8,128)S(1)} %collective-permute-done.1) | copy-start | bytes 294916
  185.6 9.1 %collective-permute-start.3 = (f32[128,12,16]{0,2,1:T(8,128)}, f32[128,12,16]{0,2,1:T(8,128)S(1)}, u32[]{:S(2)}, u32[]{:S(2)}) collective-permute-start(f32[128,12,16]{0,2,1:T(8,128)} %copy.192), channel_id=1, source_target_pairs={{2,0},{3,1},{4,2},{5,3},{6,4},{7,5},{10,8},{11,9},{12,10},{13,11},... | collective-permute-start | bytes 294920 | tf_op jit(solution)/shard_map/ppermute | solution.py:16
  189.4 0.6 copy-start.13
  190.0 17.4 %copy-start.7 = (bf16[1280,256]{1,0:T(8,128)(2,1)S(1)}, bf16[1280,256]{1,0:T(8,128)(2,1)}, u32[]{:S(2)}) copy-start(bf16[1280,256]{1,0:T(8,128)(2,1)} %param.20) | copy-start | bytes 1966084
  201.7 12.0 %all-to-all-start = ((bf16[16,2,3840]{2,1,0:T(2,128)(2,1)}), bf16[16,2,3840]{2,1,0:T(2,128)(2,1)S(1)}, u32[]{:S(2)}, u32[]{:S(2)}) async-start(bf16[16,2,3840]{2,1,0:T(2,128)(2,1)} %reshape.102), calls=%async_computation | async-start | bytes 491520 | tf_op jit(solution)/shard_map/all_to_all | solution.py:177
  207.4 7.7 %copy-start.15 = (f32[256]{0:T(256)S(1)}, f32[256]{0:T(256)}, u32[]{:S(2)}) copy-start(f32[256]{0:T(256)} %param.21) | copy-start | bytes 3076
  207.5 25.2 %copy-start.11 = (bf16[16,24,256]{2,1,0:T(8,128)(2,1)S(1)}, bf16[16,24,256]{2,1,0:T(8,128)(2,1)}, u32[]{:S(2)}) copy-start(bf16[16,24,256]{2,1,0:T(8,128)(2,1)} %param.15) | copy-start | bytes 589828
  207.5 25.2 %copy-start.14 = (bf16[256,48]{0,1:T(8,128)(2,1)S(1)}, bf16[256,48]{0,1:T(8,128)(2,1)}, u32[]{:S(2)}) copy-start(bf16[256,48]{0,1:T(8,128)(2,1)} %param.22) | copy-start | bytes 73732
  207.5 25.2 %copy-start.16 = (f32[48]{0:T(128)S(1)}, f32[48]{0:T(128)}, u32[]{:S(2)}) copy-start(f32[48]{0:T(128)} %param.23) | copy-start | bytes 580
  215.4 5.9 %collective-permute-start.6 = (bf16[1,12,256]{2,1,0:T(8,128)(2,1)S(1)}, bf16[1,12,256]{2,1,0:T(8,128)(2,1)S(1)}, u32[]{:S(2)}, u32[]{:S(2)}) collective-permute-start(bf16[1,12,256]{2,1,0:T(8,128)(2,1)S(1)} %get-tuple-element.77), channel_id=1, source_target_pairs={{0,8},{8,16},{16,24},{24,32},{32,40},{40,48},{48,56},{56,64},{64,7... | collective-permute-start | bytes 18440 | tf_op jit(solution)/shard_map/ppermute | solution.py:32
  219.1 7.7 %collective-permute-start.7 = (bf16[1,12,256]{2,1,0:T(8,128)(2,1)S(1)}, bf16[1,12,256]{2,1,0:T(8,128)(2,1)S(1)}, u32[]{:S(2)}, u32[]{:S(2)}) collective-permute-start(bf16[1,12,256]{2,1,0:T(8,128)(2,1)S(1)} %get-tuple-element.76), channel_id=1, source_target_pairs={{8,0},{16,8},{24,16},{32,24},{40,32},{48,40},{56,48},{64,56},{72,6... | collective-permute-start | bytes 18440 | tf_op jit(solution)/shard_map/ppermute | solution.py:33
  226.8 6.3 %collective-permute-start.8 = (bf16[10,1,256]{2,1,0:T(2,128)(2,1)S(1)}, bf16[10,1,256]{2,1,0:T(2,128)(2,1)S(1)}, u32[]{:S(2)}, u32[]{:S(2)}) collective-permute-start(bf16[10,1,256]{2,1,0:T(2,128)(2,1)S(1)} %get-tuple-element.74), channel_id=1, source_target_pairs={{0,1},{1,2},{2,3},{3,4},{4,5},{5,6},{6,7},{8,9},{9,10},{10,11},{11... | collective-permute-start | bytes 15368 | tf_op jit(solution)/shard_map/ppermute | solution.py:32
  228.7 5.6 %collective-permute-start.9 = (bf16[10,1,256]{2,1,0:T(2,128)(2,1)S(1)}, bf16[10,1,256]{2,1,0:T(2,128)(2,1)S(1)}, u32[]{:S(2)}, u32[]{:S(2)}) collective-permute-start(bf16[10,1,256]{2,1,0:T(2,128)(2,1)S(1)} %get-tuple-element.75), channel_id=1, source_target_pairs={{1,0},{2,1},{3,2},{4,3},{5,4},{6,5},{7,6},{9,8},{10,9},{11,10},{12... | collective-permute-start | bytes 15368 | tf_op jit(solution)/shard_map/ppermute | solution.py:33
  233.0 1.6 copy-start.6
  235.1 6.8 %collective-permute-start.10 = (bf16[1,24,304]{2,0,1:T(2,128)(2,1)S(1)}, bf16[1,24,304]{2,0,1:T(2,128)(2,1)S(1)}, u32[]{:S(2)}, u32[]{:S(2)}) collective-permute-start(bf16[1,24,304]{2,0,1:T(2,128)(2,1)S(1)} %get-tuple-element.56), channel_id=1, source_target_pairs={{0,8},{8,16},{16,24},{24,32},{32,40},{40,48},{48,56},{56,64},{64,7... | collective-permute-start | bytes 43784 | tf_op jit(solution)/shard_map/ppermute | solution.py:32
  237.1 8.0 %collective-permute-start.11 = (bf16[1,24,304]{2,0,1:T(2,128)(2,1)S(1)}, bf16[1,24,304]{2,0,1:T(2,128)(2,1)S(1)}, u32[]{:S(2)}, u32[]{:S(2)}) collective-permute-start(bf16[1,24,304]{2,0,1:T(2,128)(2,1)S(1)} %get-tuple-element.57), channel_id=1, source_target_pairs={{8,0},{16,8},{24,16},{32,24},{40,32},{48,40},{56,48},{64,56},{72,6... | collective-permute-start | bytes 43784 | tf_op jit(solution)/shard_map/ppermute | solution.py:33
  245.1 6.5 %collective-permute-start.13 = (bf16[18,1,304]{2,0,1:T(8,128)(2,1)S(1)}, bf16[18,1,304]{2,0,1:T(8,128)(2,1)S(1)}, u32[]{:S(2)}, u32[]{:S(2)}) collective-permute-start(bf16[18,1,304]{2,0,1:T(8,128)(2,1)S(1)} %get-tuple-element.46), channel_id=1, source_target_pairs={{1,0},{2,1},{3,2},{4,3},{5,4},{6,5},{7,6},{9,8},{10,9},{11,10},{12... | collective-permute-start | bytes 32840 | tf_op jit(solution)/shard_map/ppermute | solution.py:33
  249.2 5.7 %collective-permute-start.12 = (bf16[18,1,304]{2,0,1:T(8,128)(2,1)S(1)}, bf16[18,1,304]{2,0,1:T(8,128)(2,1)S(1)}, u32[]{:S(2)}, u32[]{:S(2)}) collective-permute-start(bf16[18,1,304]{2,0,1:T(8,128)(2,1)S(1)} %get-tuple-element.47), channel_id=1, source_target_pairs={{0,1},{1,2},{2,3},{3,4},{4,5},{5,6},{6,7},{8,9},{9,10},{10,11},{11... | collective-permute-start | bytes 32840 | tf_op jit(solution)/shard_map/ppermute | solution.py:32
  256.8 5.0 %copy-start.20 = (f32[256]{0:T(256)S(1)}, f32[256]{0:T(256)}, u32[]{:S(2)}) copy-start(f32[256]{0:T(256)} %param.25) | copy-start | bytes 3076
  264.1 5.9 %collective-permute-start.14 = (bf16[1,24,256]{2,1,0:T(8,128)(2,1)S(1)}, bf16[1,24,256]{2,1,0:T(8,128)(2,1)S(1)}, u32[]{:S(2)}, u32[]{:S(2)}) collective-permute-start(bf16[1,24,256]{2,1,0:T(8,128)(2,1)S(1)} %get-tuple-element.66), channel_id=1, source_target_pairs={{0,8},{8,16},{16,24},{24,32},{32,40},{40,48},{48,56},{56,64},{64,7... | collective-permute-start | bytes 36872 | tf_op jit(solution)/shard_map/ppermute | solution.py:32
  266.0 7.7 %collective-permute-start.15 = (bf16[1,24,256]{2,1,0:T(8,128)(2,1)S(1)}, bf16[1,24,256]{2,1,0:T(8,128)(2,1)S(1)}, u32[]{:S(2)}, u32[]{:S(2)}) collective-permute-start(bf16[1,24,256]{2,1,0:T(8,128)(2,1)S(1)} %get-tuple-element.67), channel_id=1, source_target_pairs={{8,0},{16,8},{24,16},{32,24},{40,32},{48,40},{56,48},{64,56},{72,6... | collective-permute-start | bytes 36872 | tf_op jit(solution)/shard_map/ppermute | solution.py:33
  273.7 5.9 %collective-permute-start.17 = (bf16[18,1,256]{2,1,0:T(2,128)(2,1)S(1)}, bf16[18,1,256]{2,1,0:T(2,128)(2,1)S(1)}, u32[]{:S(2)}, u32[]{:S(2)}) collective-permute-start(bf16[18,1,256]{2,1,0:T(2,128)(2,1)S(1)} %get-tuple-element.62), channel_id=1, source_target_pairs={{1,0},{2,1},{3,2},{4,3},{5,4},{6,5},{7,6},{9,8},{10,9},{11,10},{12... | collective-permute-start | bytes 27656 | tf_op jit(solution)/shard_map/ppermute | solution.py:33
  277.3 5.7 %collective-permute-start.16 = (bf16[18,1,256]{2,1,0:T(2,128)(2,1)S(1)}, bf16[18,1,256]{2,1,0:T(2,128)(2,1)S(1)}, u32[]{:S(2)}, u32[]{:S(2)}) collective-permute-start(bf16[18,1,256]{2,1,0:T(2,128)(2,1)S(1)} %get-tuple-element.63), channel_id=1, source_target_pairs={{0,1},{1,2},{2,3},{3,4},{4,5},{5,6},{6,7},{8,9},{9,10},{10,11},{11... | collective-permute-start | bytes 27656 | tf_op jit(solution)/shard_map/ppermute | solution.py:32
  283.2 1.3 copy-start.18
  283.2 1.3 copy-start.21
Sparse Core Ops, SparseCore 0:
  9.8 68.4 all-gather.1
where the time goes:
time: 295 us; the launch traced here: 293 us
  local copies, waits for them, and re-layouts  84.3 us (29%)
  starting transfers between devices  63.8 us (22%)
  blocking collectives  60.8 us (21%)
  waiting for transfers between devices  36.8 us (12%)
  other arithmetic  20.4 us (7%)
  between operations  14.2 us (5%)
  matrix products  12.4 us (4%)
    psum x3, blocking collectives, one_axis_at_a_time(): value = lax.psum(value, axis)  60.8 us
    ppermute x6, starting transfers between devices, from_behind(): return lax.ppermute(value, axis, pairs)  22.8 us
    unnamed x66, local copies, waits for them, and re-layouts  22.7 us
    ppermute x6, starting transfers between devices, padded_2(): after = lax.ppermute(first, axis, down)  21.6 us
    ppermute x6, starting transfers between devices, padded_2(): before = lax.ppermute(last, axis, up)  13.6 us
    slice x1, local copies, waits for them, and re-layouts, group(): return products[:, :, number * own_width:(number + 1) * own_width]  13.5 us
    ppermute x6, waiting for transfers between devices, padded_2(): after = lax.ppermute(first, axis, down)  13.4 us
    reshape x1, local copies, waits for them, and re-layouts, on_device(): piece.reshape(-1, in_width)  10.8 us
  transfers between devices with their start and end apart: 20, of which 9 were waited for; matrix products, arithmetic and copies ran while one was open for 4% of the time, Pallas kernels for 0%

commit v1 on v0

--- a/solution.py
+++ b/solution.py
@@ -131,7 +131,9 @@
     own_stack = jnp.concatenate([point_weight, atrous_flat, pool_weight], axis=1)
     group_total = 28
     stacked = own_stack[:, : group_total * own_width]
-    piece = lax.all_gather(features, ROW, axis=0, tiled=True)
+    piece = jnp.concatenate(
+        lax.all_to_all(jnp.stack([features] * lax.axis_size(ROW)), ROW, 0, 0), axis=0
+    )
     result = jnp.dot(piece.reshape(-1, in_width), stacked, preferred_element_type=jnp.float32)
     products = result.reshape(piece.shape[0], piece.shape[1], -1)
     map_rows = products.shape[0]

time: 295 us -> 351 us (1.19)
  blocking collectives: 60.8 us -> 128 us
  between operations: 14.2 us -> 0.81 us
  waiting for transfers between devices: 36.8 us -> 26.6 us
  starting transfers between devices: 63.8 us -> 72.9 us
  local copies, waits for them, and re-layouts: 84.3 us -> 90.7 us
    psum x3, blocking collectives: 60.8 us -> 128 us  [one_axis_at_a_time(): value = lax.psum(value, axis)]
    another operation x0 -> x2, local copies, waits for them, and re-layouts: none -> 15.4 us  [the longest x1 10.8 us: on_device(): piece.reshape(-1, in_width)]
    all_to_all x0 -> x1, local copies, waits for them, and re-layouts: none -> 11.5 us  [on_device(): lax.all_to_all(jnp.stack([features] * lax.axis_size(ROW)), ROW, 0, 0)]
    reshape x1 -> x0, local copies, waits for them, and re-layouts: 10.8 us -> none  [on_device(): piece.reshape(-1, in_width)]
    all_gather x1 -> x0, local copies, waits for them, and re-layouts: 9.74 us -> none  [on_device(): piece = lax.all_gather(features, ROW, axis=0, tiled=True)]
    all_to_all x0 -> x1, starting transfers between devices: none -> 7.55 us  [on_device(): lax.all_to_all(jnp.stack([features] * lax.axis_size(ROW)), ROW, 0, 0)]
    all_gather x1 -> x0, waiting for transfers between devices: 7.23 us -> none  [on_device(): piece = lax.all_gather(features, ROW, axis=0, tiled=True)]
    unnamed x66 -> x72, local copies, waits for them, and re-layouts: 22.7 us -> 22.7 us
  transfers between devices with their start and end apart: 20 -> 20, of which waited for: 9 -> 8; matrix products, arithmetic and copies ran while one was open for 4% -> 2% of each run, Pallas kernels for 0% -> 0%
where the time goes in v1:
time: 351 us; the launch traced here: 349 us
  blocking collectives  128 us (36%)
  local copies, waits for them, and re-layouts  90.7 us (26%)
  starting transfers between devices  72.9 us (21%)
  waiting for transfers between devices  26.6 us (8%)
  other arithmetic  18.6 us (5%)
  matrix products  11.6 us (3%)
    psum x3, blocking collectives, one_axis_at_a_time(): value = lax.psum(value, axis)  128 us
    ppermute x6, starting transfers between devices, from_behind(): return lax.ppermute(value, axis, pairs)  22.8 us
    unnamed x72, local copies, waits for them, and re-layouts  22.7 us
    ppermute x6, starting transfers between devices, padded_2(): after = lax.ppermute(first, axis, down)  20.3 us
    ppermute x6, starting transfers between devices, padded_2(): before = lax.ppermute(last, axis, up)  15 us
    ppermute x6, waiting for transfers between devices, padded_2(): after = lax.ppermute(first, axis, down)  13.5 us
    slice x1, local copies, waits for them, and re-layouts, group(): return products[:, :, number * own_width:(number + 1) * own_width]  13.5 us
    all_to_all x1, local copies, waits for them, and re-layouts, on_device(): lax.all_to_all(jnp.stack([features] * lax.axis_size(ROW)), ROW, 0, 0)  11.5 us
  transfers between devices with their start and end apart: 20, of which 8 were waited for; matrix products, arithmetic and copies ran while one was open for 2% of the time, Pallas kernels for 0%

profile of v1, /device:TPU:70, one launch (start us, length us, event | category | flops | bytes accessed | tf_op | source)
XLA Modules:
  0.0 349.2 jit_solution(13149293095165722410)
XLA Ops:
  0.0 4.6 %stack.14 = bf16[16,8,12,2048]{3,1,2,0:T(8,128)(2,1)} broadcast(bf16[8,12,2048]{2,0,1:T(8,128)(2,1)} %param.14), dimensions={1,2,3} | broadcast | bytes 6684672 | tf_op jit(solution)/shard_map/stack | solution.py:135
  4.6 7.6 %all-to-all-start = ((bf16[16,8,12,2048]{3,1,2,0:T(8,128)(2,1)}), bf16[16,8,12,2048]{3,1,2,0:T(8,128)(2,1)}, u32[]{:S(2)}, u32[]{:S(2)}) async-start(bf16[16,8,12,2048]{3,1,2,0:T(8,128)(2,1)} %stack.14), calls=%async_computation | async-start | bytes 12582912 | tf_op jit(solution)/shard_map/all_to_all | solution.py:135
  12.6 79.6 %all-reduce.20 = (f32[5,256]{1,0:T(8,128)S(1)}, f32[2048]{0:T(1024)S(1)}) all-reduce(f32[5,256]{1,0:T(8,128)S(1)} %dynamic_update_slice.3, f32[2048]{0:T(1024)S(1)} %convert_reduce_fusion), channel_id=1, replica_groups=mesh['dp'=2,'row_0'=4,'row_1'=4,'col'=8] {'row_0'}, use_global_device_ids=true, to_apply=%region_0.1 | all-reduce | flops 3328 | bytes 26624 | tf_op jit(solution)/shard_map/psum | solution.py:21
  92.2 18.8 %all-reduce.19 = (f32[5,256]{1,0:T(8,128)S(1)}, f32[2048]{0:T(1024)S(1)}) all-reduce(f32[5,256]{1,0:T(8,128)S(1)} %get-tuple-element.9, f32[2048]{0:T(1024)S(1)} %get-tuple-element.10), channel_id=1, replica_groups=mesh['dp'=2,'row_0'=4,'row_1'=4,'col'=8] {'row_1'}, use_global_device_ids=true, to_apply=%region_1.2 | all-reduce | flops 3328 | bytes 26624 | tf_op jit(solution)/shard_map/psum | solution.py:21
  110.9 29.7 %all-reduce.18 = (f32[5,256]{1,0:T(8,128)S(1)}, f32[2048]{0:T(1024)S(1)}) all-reduce(f32[5,256]{1,0:T(8,128)S(1)} %get-tuple-element.7, f32[2048]{0:T(1024)S(1)} %get-tuple-element.8), channel_id=1, replica_groups=mesh['dp'=2,'row_0'=4,'row_1'=4,'col'=8] {'col'}, use_global_device_ids=true, to_apply=%region_2.3 | all-reduce | flops 3328 | bytes 26624 | tf_op jit(solution)/shard_map/psum | solution.py:21
  140.9 11.5 %copy.181 = bf16[16,8,12,2048]{3,2,1,0:T(8,128)(2,1)} copy(bf16[16,8,12,2048]{3,1,2,0:T(8,128)(2,1)} %all-to-all-done) | data formatting | bytes 12582912 | tf_op jit(solution)/shard_map/all_to_all | solution.py:135
  152.3 10.8 %reshape_reshape.3 = bf16[1536,2048]{1,0:T(8,128)(2,1)} reshape(bf16[16,8,12,2048]{3,2,1,0:T(8,128)(2,1)} %copy.181) | data formatting | bytes 12582912 | tf_op jit(solution)/shard_map/reshape;reshape | solution.py:137
  163.2 7.3 %convolution_bitcast_fusion = f32[1536,448]{0,1:T(8,128)} fusion(bf16[1536,2048]{1,0:T(8,128)(2,1)} %reshape_reshape.3, bf16[2048,432]{0,1:T(8,128)(2,1)S(1)} %bitcast.118, bf16[2048,16]{0,1:T(8,128)(2,1)S(1)} %copy-done.22), kind=kOutput, calls=%fused_computation | convolution fusion | flops 2822242304 | bytes 10878976 | tf_op jit(solution)/shard_map/dot_general | solution.py:137
  170.5 3.5 copy.182
  174.0 4.6 %reshape.86 = f32[128,12,448]{2,1,0:T(8,128)} reshape(f32[1536,448]{1,0:T(8,128)} %copy.182) | data formatting | bytes 5505024 | tf_op jit(solution)/shard_map/reshape | solution.py:138
  178.6 13.5 %fusion.61 = (f32[128,12,16]{2,1,0:T(8,128)}, f32[128,12,16]{2,1,0:T(8,128)}, f32[128,12,16]{2,1,0:T(8,128)}, f32[128,12,16]{2,1,0:T(8,128)}, f32[128,12,16]{2,1...) fusion(f32[128,12,448]{2,1,0:T(8,128)} %reshape.86), kind=kLoop, calls=%fused_computation.144 | loop fusion | bytes 3735552 | tf_op jit(solution)/shard_map/slice | solution.py:142
  192.0 2.2 copy.225
  194.2 2.1 copy.226
  196.3 2.2 copy.224
  198.5 2.2 copy.223
  200.7 2.2 copy.222
  202.8 2.2 copy.221
  205.0 2.2 copy.220
  209.3 8.6 %fusion.62 = (f32[128,12,16]{2,1,0:T(8,128)}, f32[128,12,16]{2,1,0:T(8,128)}, f32[128,12,16]{2,1,0:T(8,128)}, f32[128,12,16]{2,1,0:T(8,128)}, f32[128,12,16]{2,1...) fusion(f32[128,12,448]{2,1,0:T(8,128)} %reshape.86, ...), kind=kLoop, calls=%fused_computation.145 | loop fusion | flops 245760 | bytes 2555904 | tf_op jit(solution)/shard_map/slice | solution.py:142
  222.8 2.2 copy.189
  225.0 2.1 copy.188
  229.5 1.9 collective-permute-start.1
  231.5 9.3 %collective-permute-start.2 = (f32[128,12,16]{0,2,1:T(8,128)}, f32[128,12,16]{0,2,1:T(8,128)}, u32[]{:S(2)}, u32[]{:S(2)}) collective-permute-start(f32[128,12,16]{0,2,1:T(8,128)} %copy.189), channel_id=1, source_target_pairs={{0,2},{1,3},{2,4},{3,5},{4,6},{5,7},{8,10},{9,11},{10,12},{11,13},... | collective-permute-start | bytes 294920 | tf_op jit(solution)/shard_map/ppermute | solution.py:16
  240.8 2.7 collective-permute-start.4
  243.4 1.9 collective-permute-start
  248.0 5.6 %collective-permute-start.3 = (f32[128,12,16]{0,2,1:T(8,128)}, f32[128,12,16]{0,2,1:T(8,128)S(1)}, u32[]{:S(2)}, u32[]{:S(2)}) collective-permute-start(f32[128,12,16]{0,2,1:T(8,128)} %copy.193), channel_id=1, source_target_pairs={{2,0},{3,1},{4,2},{5,3},{6,4},{7,5},{10,8},{11,9},{12,10},{13,11},... | collective-permute-start | bytes 294920 | tf_op jit(solution)/shard_map/ppermute | solution.py:16
  254.2 1.9 fusion.59
  264.9 7.3 %all-to-all-start.1 = ((bf16[16,2,3840]{2,1,0:T(2,128)(2,1)}), bf16[16,2,3840]{2,1,0:T(2,128)(2,1)S(1)}, u32[]{:S(2)}, u32[]{:S(2)}) async-start(bf16[16,2,3840]{2,1,0:T(2,128)(2,1)} %reshape.100), calls=%async_computation.1 | async-start | bytes 491520 | tf_op jit(solution)/shard_map/all_to_all | solution.py:179
  272.2 6.2 %all-to-all-done.1 = bf16[16,2,3840]{2,1,0:T(2,128)(2,1)S(1)} async-done(((bf16[16,2,3840]{2,1,0:T(2,128)(2,1)}), bf16[16,2,3840]{2,1,0:T(2,128)(2,1)S(1)}, u32[]{:S(2)}, u32[]{:S(2)}) %all-to-all-start.1) | async-done | bytes 245792 | tf_op jit(solution)/shard_map/all_to_all | solution.py:179
  280.2 3.6 %collective-permute-start.6 = (bf16[1,12,256]{2,1,0:T(8,128)(2,1)S(1)}, bf16[1,12,256]{2,1,0:T(8,128)(2,1)S(1)}, u32[]{:S(2)}, u32[]{:S(2)}) collective-permute-start(bf16[1,12,256]{2,1,0:T(8,128)(2,1)S(1)} %get-tuple-element.77), channel_id=1, source_target_pairs={{0,8},{8,16},{16,24},{24,32},{32,40},{40,48},{48,56},{56,64},{64,7... | collective-permute-start | bytes 18440 | tf_op jit(solution)/shard_map/ppermute | solution.py:32
  283.8 2.2 collective-permute-start.7
  286.1 5.5 %collective-permute-done.7 = bf16[1,12,256]{2,1,0:T(8,128)(2,1)S(1)} collective-permute-done((bf16[1,12,256]{2,1,0:T(8,128)(2,1)S(1)}, bf16[1,12,256]{2,1,0:T(8,128)(2,1)S(1)}, u32[]{:S(2)}, u32[]{:S(2)}) %collective-permute-start.7) | collective-permute-done | bytes 6176 | tf_op jit(solution)/shard_map/ppermute | solution.py:33
  291.6 1.9 collective-permute-start.8
  293.5 3.9 %collective-permute-start.9 = (bf16[10,1,256]{2,1,0:T(2,128)(2,1)S(1)}, bf16[10,1,256]{2,1,0:T(2,128)(2,1)S(1)}, u32[]{:S(2)}, u32[]{:S(2)}) collective-permute-start(bf16[10,1,256]{2,1,0:T(2,128)(2,1)S(1)} %get-tuple-element.75), channel_id=1, source_target_pairs={{1,0},{2,1},{3,2},{4,3},{5,4},{6,5},{7,6},{9,8},{10,9},{11,10},{12... | collective-permute-start | bytes 15368 | tf_op jit(solution)/shard_map/ppermute | solution.py:33
  299.9 1.9 collective-permute-start.10
  301.8 3.9 %collective-permute-start.11 = (bf16[1,24,304]{2,0,1:T(2,128)(2,1)S(1)}, bf16[1,24,304]{2,0,1:T(2,128)(2,1)S(1)}, u32[]{:S(2)}, u32[]{:S(2)}) collective-permute-start(bf16[1,24,304]{2,0,1:T(2,128)(2,1)S(1)} %get-tuple-element.57), channel_id=1, source_target_pairs={{8,0},{16,8},{24,16},{32,24},{40,32},{48,40},{56,48},{64,56},{72,6... | collective-permute-start | bytes 43784 | tf_op jit(solution)/shard_map/ppermute | solution.py:33
  306.7 3.1 collective-permute-done.11
  309.8 4.1 %collective-permute-start.13 = (bf16[18,1,304]{2,0,1:T(8,128)(2,1)S(1)}, bf16[18,1,304]{2,0,1:T(8,128)(2,1)S(1)}, u32[]{:S(2)}, u32[]{:S(2)}) collective-permute-start(bf16[18,1,304]{2,0,1:T(8,128)(2,1)S(1)} %get-tuple-element.46), channel_id=1, source_target_pairs={{1,0},{2,1},{3,2},{4,3},{5,4},{6,5},{7,6},{9,8},{10,9},{11,10},{12... | collective-permute-start | bytes 32840 | tf_op jit(solution)/shard_map/ppermute | solution.py:33
  314.0 1.9 collective-permute-start.12
  316.3 3.3 collective-permute-done.12
  321.5 4.9 %concatenate.122 = bf16[384,2736]{1,0:T(8,128)(2,1)} concatenate(bf16[384,304]{1,0:T(8,128)(2,1)S(1)} %bitcast.104, bf16[384,304]{1,0:T(8,128)(2,1)S(1)} %bitcast.100, bf16[384,304]{1,0:T(8,128)(2,1)S(1)} %bitcast.103, bf16[384,304]{1,0:T(8,128)(2,1)S(1)} %bitcast.105, bf16[384,256]{1,0:T(8,128)(2,1)} %convert_element_type.76, bf16[384,48]{1,0:T(8,128)(2,1)} %copy-done.7, ...), dimensions={1} | concatenate | bytes 4202496 | tf_op jit(solution)/shard_map/concatenate | solution.py:61
  326.5 2.3 fusion.6
  328.8 1.9 collective-permute-start.14
  330.8 3.9 %collective-permute-start.15 = (bf16[1,24,256]{2,1,0:T(8,128)(2,1)S(1)}, bf16[1,24,256]{2,1,0:T(8,128)(2,1)S(1)}, u32[]{:S(2)}, u32[]{:S(2)}) collective-permute-start(bf16[1,24,256]{2,1,0:T(8,128)(2,1)S(1)} %get-tuple-element.67), channel_id=1, source_target_pairs={{8,0},{16,8},{24,16},{32,24},{40,32},{48,40},{56,48},{64,56},{72,6... | collective-permute-start | bytes 36872 | tf_op jit(solution)/shard_map/ppermute | solution.py:33
  334.7 3.8 %collective-permute-done.15 = bf16[1,24,256]{2,1,0:T(8,128)(2,1)S(1)} collective-permute-done((bf16[1,24,256]{2,1,0:T(8,128)(2,1)S(1)}, bf16[1,24,256]{2,1,0:T(8,128)(2,1)S(1)}, u32[]{:S(2)}, u32[]{:S(2)}) %collective-permute-start.15) | collective-permute-done | bytes 12320 | tf_op jit(solution)/shard_map/ppermute | solution.py:33
  338.5 2.2 collective-permute-start.17
  340.7 3.7 %collective-permute-start.16 = (bf16[18,1,256]{2,1,0:T(2,128)(2,1)S(1)}, bf16[18,1,256]{2,1,0:T(2,128)(2,1)S(1)}, u32[]{:S(2)}, u32[]{:S(2)}) collective-permute-start(bf16[18,1,256]{2,1,0:T(2,128)(2,1)S(1)} %get-tuple-element.63), channel_id=1, source_target_pairs={{0,1},{1,2},{2,3},{3,4},{4,5},{5,6},{6,7},{8,9},{9,10},{10,11},{11... | collective-permute-start | bytes 27656 | tf_op jit(solution)/shard_map/ppermute | solution.py:32
  344.4 1.9 collective-permute-done.16
  (145 shorter events, 32.2 us)
Async XLA Ops:
  0.0 326.5 %copy-start = (bf16[3,3,304,256]{3,2,1,0:T(8,128)(2,1)S(1)}, bf16[3,3,304,256]{3,2,1,0:T(8,128)(2,1)}, u32[]{:S(2)}) copy-start(bf16[3,3,304,256]{3,2,1,0:T(8,128)(2,1)} %param.24) | copy-start | bytes 4202500
  4.6 7.6 %copy-start.16 = (f32[5,16]{1,0:T(8,128)S(1)}, f32[5,16]{1,0:T(8,128)}, u32[]{:S(2)}) copy-start(f32[5,16]{1,0:T(8,128)} %param.19) | copy-start | bytes 964
  4.6 7.9 %copy-start.6 = (bf16[8,12,2048]{2,0,1:T(8,128)(2,1)S(1)}, bf16[8,12,2048]{2,0,1:T(8,128)(2,1)}, u32[]{:S(2)}) copy-start(bf16[8,12,2048]{2,0,1:T(8,128)(2,1)} %param.14) | copy-start | bytes 1179652
  4.6 136.1 %copy-start.21 = (bf16[2048,16]{0,1:T(8,128)(2,1)S(1)}, bf16[2048,16]{0,1:T(8,128)(2,1)}, u32[]{:S(2)}) copy-start(bf16[2048,16]{0,1:T(8,128)(2,1)} %param.18) | copy-start | bytes 196612
  4.6 136.3 %all-to-all-start = ((bf16[16,8,12,2048]{3,1,2,0:T(8,128)(2,1)}), bf16[16,8,12,2048]{3,1,2,0:T(8,128)(2,1)}, u32[]{:S(2)}, u32[]{:S(2)}) async-start(bf16[16,8,12,2048]{3,1,2,0:T(8,128)(2,1)} %stack.14), calls=%async_computation | async-start | bytes 12582912 | tf_op jit(solution)/shard_map/all_to_all | solution.py:135
  152.3 10.8 %copy-start.19 = (bf16[3,3,3,2048,16]{3,4,2,1,0:T(8,128)(2,1)S(1)}, bf16[3,3,3,2048,16]{3,4,2,1,0:T(8,128)(2,1)}, u32[]{:S(2)}) copy-start(bf16[3,3,3,2048,16]{3,4,2,1,0:T(8,128)(2,1)} %param.17) | copy-start | bytes 5308420
  152.3 10.8 %copy-start.22 = (bf16[2048,16]{0,1:T(8,128)(2,1)S(1)}, bf16[2048,16]{0,1:T(8,128)(2,1)}, u32[]{:S(2)}) copy-start(bf16[2048,16]{0,1:T(8,128)(2,1)} %param.16) | copy-start | bytes 196612
  208.1 1.2 copy-start.1
  217.9 2.6 copy-start.5
  220.6 1.2 copy-start.4
  221.6 5.6 %copy-start.3 = (f32[128,12,16]{2,1,0:T(8,128)S(1)}, f32[128,12,16]{2,1,0:T(8,128)}, u32[]{:S(2)}) copy-start(f32[128,12,16]{2,1,0:T(8,128)} %get-tuple-element.35) | copy-start | bytes 294916
  222.8 24.2 %copy-start.2 = (f32[128,12,16]{2,1,0:T(8,128)S(1)}, f32[128,12,16]{2,1,0:T(8,128)}, u32[]{:S(2)}) copy-start(f32[128,12,16]{2,1,0:T(8,128)} %get-tuple-element.31) | copy-start | bytes 294916
  228.1 29.7 %copy-start.11 = (f32[128,12,16]{0,2,1:T(8,128)S(1)}, f32[128,12,16]{0,2,1:T(8,128)}, u32[]{:S(2)}) copy-start(f32[128,12,16]{0,2,1:T(8,128)} %copy.224) | copy-start | bytes 294916
  228.1 31.5 %copy-start.9 = (f32[128,12,16]{0,2,1:T(8,128)S(1)}, f32[128,12,16]{0,2,1:T(8,128)}, u32[]{:S(2)}) copy-start(f32[128,12,16]{0,2,1:T(8,128)} %copy.225) | copy-start | bytes 294916
  228.1 31.5 %copy-start.10 = (f32[128,12,16]{0,2,1:T(8,128)S(1)}, f32[128,12,16]{0,2,1:T(8,128)}, u32[]{:S(2)}) copy-start(f32[128,12,16]{0,2,1:T(8,128)} %copy.226) | copy-start | bytes 294916
  228.1 31.5 %collective-permute-start.5 = (f32[128,12,16]{0,2,1:T(8,128)}, f32[128,12,16]{0,2,1:T(8,128)}, u32[]{:S(2)}, u32[]{:S(2)}) collective-permute-start(f32[128,12,16]{0,2,1:T(8,128)} %copy.198), channel_id=1, source_target_pairs={{3,0},{4,1},{5,2},{6,3},{7,4},{11,8},{12,9},{13,10},{14,11},{15,12... | collective-permute-start | bytes 294920 | tf_op jit(solution)/shard_map/ppermute | solution.py:16
  229.5 18.4 %collective-permute-start.1 = (f32[128,12,16]{0,2,1:T(8,128)}, f32[128,12,16]{0,2,1:T(8,128)S(1)}, u32[]{:S(2)}, u32[]{:S(2)}) collective-permute-start(f32[128,12,16]{0,2,1:T(8,128)} %copy.188), channel_id=1, source_target_pairs={{1,0},{2,1},{3,2},{4,3},{5,4},{6,5},{7,6},{9,8},{10,9},{11,10},{12... | collective-permute-start | bytes 294920 | tf_op jit(solution)/shard_map/ppermute | solution.py:16
  231.5 24.6 %collective-permute-start.2 = (f32[128,12,16]{0,2,1:T(8,128)}, f32[128,12,16]{0,2,1:T(8,128)}, u32[]{:S(2)}, u32[]{:S(2)}) collective-permute-start(f32[128,12,16]{0,2,1:T(8,128)} %copy.189), channel_id=1, source_target_pairs={{0,2},{1,3},{2,4},{3,5},{4,6},{5,7},{8,10},{9,11},{10,12},{11,13},... | collective-permute-start | bytes 294920 | tf_op jit(solution)/shard_map/ppermute | solution.py:16
  240.8 18.8 %collective-permute-start.4 = (f32[128,12,16]{0,2,1:T(8,128)}, f32[128,12,16]{0,2,1:T(8,128)}, u32[]{:S(2)}, u32[]{:S(2)}) collective-permute-start(f32[128,12,16]{0,2,1:T(8,128)} %copy.194), channel_id=1, source_target_pairs={{0,3},{1,4},{2,5},{3,6},{4,7},{8,11},{9,12},{10,13},{11,14},{12,15... | collective-permute-start | bytes 294920 | tf_op jit(solution)/shard_map/ppermute | solution.py:16
  243.4 10.1 %collective-permute-start = (f32[128,12,16]{0,2,1:T(8,128)}, f32[128,12,16]{0,2,1:T(8,128)S(1)}, u32[]{:S(2)}, u32[]{:S(2)}) collective-permute-start(f32[128,12,16]{0,2,1:T(8,128)} %copy.184), channel_id=1, source_target_pairs={{0,1},{1,2},{2,3},{3,4},{4,5},{5,6},{6,7},{8,9},{9,10},{10,11},{11... | collective-permute-start | bytes 294920 | tf_op jit(solution)/shard_map/ppermute | solution.py:16
  248.0 5.6 %copy-start.13 = (f32[128,12,16]{0,2,1:T(8,128)}, f32[128,12,16]{0,2,1:T(8,128)S(1)}, u32[]{:S(2)}) copy-start(f32[128,12,16]{0,2,1:T(8,128)S(1)} %collective-permute-done.1) | copy-start | bytes 294916
  248.0 9.9 %collective-permute-start.3 = (f32[128,12,16]{0,2,1:T(8,128)}, f32[128,12,16]{0,2,1:T(8,128)S(1)}, u32[]{:S(2)}, u32[]{:S(2)}) collective-permute-start(f32[128,12,16]{0,2,1:T(8,128)} %copy.193), channel_id=1, source_target_pairs={{2,0},{3,1},{4,2},{5,3},{6,4},{7,5},{10,8},{11,9},{12,10},{13,11},... | collective-permute-start | bytes 294920 | tf_op jit(solution)/shard_map/ppermute | solution.py:16
  253.6 0.6 copy-start.14
  254.2 17.9 %copy-start.8 = (bf16[1280,256]{1,0:T(8,128)(2,1)S(1)}, bf16[1280,256]{1,0:T(8,128)(2,1)}, u32[]{:S(2)}) copy-start(bf16[1280,256]{1,0:T(8,128)(2,1)} %param.20) | copy-start | bytes 1966084
  264.9 13.5 %all-to-all-start.1 = ((bf16[16,2,3840]{2,1,0:T(2,128)(2,1)}), bf16[16,2,3840]{2,1,0:T(2,128)(2,1)S(1)}, u32[]{:S(2)}, u32[]{:S(2)}) async-start(bf16[16,2,3840]{2,1,0:T(2,128)(2,1)} %reshape.100), calls=%async_computation.1 | async-start | bytes 491520 | tf_op jit(solution)/shard_map/all_to_all | solution.py:179
  272.1 7.7 %copy-start.17 = (f32[256]{0:T(256)S(1)}, f32[256]{0:T(256)}, u32[]{:S(2)}) copy-start(f32[256]{0:T(256)} %param.21) | copy-start | bytes 3076
  272.2 25.2 %copy-start.12 = (bf16[16,24,256]{2,1,0:T(8,128)(2,1)S(1)}, bf16[16,24,256]{2,1,0:T(8,128)(2,1)}, u32[]{:S(2)}) copy-start(bf16[16,24,256]{2,1,0:T(8,128)(2,1)} %param.15) | copy-start | bytes 589828
  272.2 25.2 %copy-start.15 = (bf16[256,48]{0,1:T(8,128)(2,1)S(1)}, bf16[256,48]{0,1:T(8,128)(2,1)}, u32[]{:S(2)}) copy-start(bf16[256,48]{0,1:T(8,128)(2,1)} %param.22) | copy-start | bytes 73732
  272.2 25.2 %copy-start.18 = (f32[48]{0:T(128)S(1)}, f32[48]{0:T(128)}, u32[]{:S(2)}) copy-start(f32[48]{0:T(128)} %param.23) | copy-start | bytes 580
  280.2 5.9 %collective-permute-start.6 = (bf16[1,12,256]{2,1,0:T(8,128)(2,1)S(1)}, bf16[1,12,256]{2,1,0:T(8,128)(2,1)S(1)}, u32[]{:S(2)}, u32[]{:S(2)}) collective-permute-start(bf16[1,12,256]{2,1,0:T(8,128)(2,1)S(1)} %get-tuple-element.77), channel_id=1, source_target_pairs={{0,8},{8,16},{16,24},{24,32},{32,40},{40,48},{48,56},{56,64},{64,7... | collective-permute-start | bytes 18440 | tf_op jit(solution)/shard_map/ppermute | solution.py:32
  283.8 7.7 %collective-permute-start.7 = (bf16[1,12,256]{2,1,0:T(8,128)(2,1)S(1)}, bf16[1,12,256]{2,1,0:T(8,128)(2,1)S(1)}, u32[]{:S(2)}, u32[]{:S(2)}) collective-permute-start(bf16[1,12,256]{2,1,0:T(8,128)(2,1)S(1)} %get-tuple-element.76), channel_id=1, source_target_pairs={{8,0},{16,8},{24,16},{32,24},{40,32},{48,40},{56,48},{64,56},{72,6... | collective-permute-start | bytes 18440 | tf_op jit(solution)/shard_map/ppermute | solution.py:33
  291.6 6.3 %collective-permute-start.8 = (bf16[10,1,256]{2,1,0:T(2,128)(2,1)S(1)}, bf16[10,1,256]{2,1,0:T(2,128)(2,1)S(1)}, u32[]{:S(2)}, u32[]{:S(2)}) collective-permute-start(bf16[10,1,256]{2,1,0:T(2,128)(2,1)S(1)} %get-tuple-element.74), channel_id=1, source_target_pairs={{0,1},{1,2},{2,3},{3,4},{4,5},{5,6},{6,7},{8,9},{9,10},{10,11},{11... | collective-permute-start | bytes 15368 | tf_op jit(solution)/shard_map/ppermute | solution.py:32
  293.5 5.6 %collective-permute-start.9 = (bf16[10,1,256]{2,1,0:T(2,128)(2,1)S(1)}, bf16[10,1,256]{2,1,0:T(2,128)(2,1)S(1)}, u32[]{:S(2)}, u32[]{:S(2)}) collective-permute-start(bf16[10,1,256]{2,1,0:T(2,128)(2,1)S(1)} %get-tuple-element.75), channel_id=1, source_target_pairs={{1,0},{2,1},{3,2},{4,3},{5,4},{6,5},{7,6},{9,8},{10,9},{11,10},{12... | collective-permute-start | bytes 15368 | tf_op jit(solution)/shard_map/ppermute | solution.py:33
  297.8 1.6 copy-start.7
  299.9 6.8 %collective-permute-start.10 = (bf16[1,24,304]{2,0,1:T(2,128)(2,1)S(1)}, bf16[1,24,304]{2,0,1:T(2,128)(2,1)S(1)}, u32[]{:S(2)}, u32[]{:S(2)}) collective-permute-start(bf16[1,24,304]{2,0,1:T(2,128)(2,1)S(1)} %get-tuple-element.56), channel_id=1, source_target_pairs={{0,8},{8,16},{16,24},{24,32},{32,40},{40,48},{48,56},{56,64},{64,7... | collective-permute-start | bytes 43784 | tf_op jit(solution)/shard_map/ppermute | solution.py:32
  301.8 8.0 %collective-permute-start.11 = (bf16[1,24,304]{2,0,1:T(2,128)(2,1)S(1)}, bf16[1,24,304]{2,0,1:T(2,128)(2,1)S(1)}, u32[]{:S(2)}, u32[]{:S(2)}) collective-permute-start(bf16[1,24,304]{2,0,1:T(2,128)(2,1)S(1)} %get-tuple-element.57), channel_id=1, source_target_pairs={{8,0},{16,8},{24,16},{32,24},{40,32},{48,40},{56,48},{64,56},{72,6... | collective-permute-start | bytes 43784 | tf_op jit(solution)/shard_map/ppermute | solution.py:33
  309.8 6.5 %collective-permute-start.13 = (bf16[18,1,304]{2,0,1:T(8,128)(2,1)S(1)}, bf16[18,1,304]{2,0,1:T(8,128)(2,1)S(1)}, u32[]{:S(2)}, u32[]{:S(2)}) collective-permute-start(bf16[18,1,304]{2,0,1:T(8,128)(2,1)S(1)} %get-tuple-element.46), channel_id=1, source_target_pairs={{1,0},{2,1},{3,2},{4,3},{5,4},{6,5},{7,6},{9,8},{10,9},{11,10},{12... | collective-permute-start | bytes 32840 | tf_op jit(solution)/shard_map/ppermute | solution.py:33
  314.0 5.7 %collective-permute-start.12 = (bf16[18,1,304]{2,0,1:T(8,128)(2,1)S(1)}, bf16[18,1,304]{2,0,1:T(8,128)(2,1)S(1)}, u32[]{:S(2)}, u32[]{:S(2)}) collective-permute-start(bf16[18,1,304]{2,0,1:T(8,128)(2,1)S(1)} %get-tuple-element.47), channel_id=1, source_target_pairs={{0,1},{1,2},{2,3},{3,4},{4,5},{5,6},{6,7},{8,9},{9,10},{10,11},{11... | collective-permute-start | bytes 32840 | tf_op jit(solution)/shard_map/ppermute | solution.py:32
  321.5 4.9 %copy-start.23 = (f32[256]{0:T(256)S(1)}, f32[256]{0:T(256)}, u32[]{:S(2)}) copy-start(f32[256]{0:T(256)} %param.25) | copy-start | bytes 3076
  328.8 5.9 %collective-permute-start.14 = (bf16[1,24,256]{2,1,0:T(8,128)(2,1)S(1)}, bf16[1,24,256]{2,1,0:T(8,128)(2,1)S(1)}, u32[]{:S(2)}, u32[]{:S(2)}) collective-permute-start(bf16[1,24,256]{2,1,0:T(8,128)(2,1)S(1)} %get-tuple-element.66), channel_id=1, source_target_pairs={{0,8},{8,16},{16,24},{24,32},{32,40},{40,48},{48,56},{56,64},{64,7... | collective-permute-start | bytes 36872 | tf_op jit(solution)/shard_map/ppermute | solution.py:32
  330.8 7.7 %collective-permute-start.15 = (bf16[1,24,256]{2,1,0:T(8,128)(2,1)S(1)}, bf16[1,24,256]{2,1,0:T(8,128)(2,1)S(1)}, u32[]{:S(2)}, u32[]{:S(2)}) collective-permute-start(bf16[1,24,256]{2,1,0:T(8,128)(2,1)S(1)} %get-tuple-element.67), channel_id=1, source_target_pairs={{8,0},{16,8},{24,16},{32,24},{40,32},{48,40},{56,48},{64,56},{72,6... | collective-permute-start | bytes 36872 | tf_op jit(solution)/shard_map/ppermute | solution.py:33
  338.5 5.9 %collective-permute-start.17 = (bf16[18,1,256]{2,1,0:T(2,128)(2,1)S(1)}, bf16[18,1,256]{2,1,0:T(2,128)(2,1)S(1)}, u32[]{:S(2)}, u32[]{:S(2)}) collective-permute-start(bf16[18,1,256]{2,1,0:T(2,128)(2,1)S(1)} %get-tuple-element.62), channel_id=1, source_target_pairs={{1,0},{2,1},{3,2},{4,3},{5,4},{6,5},{7,6},{9,8},{10,9},{11,10},{12... | collective-permute-start | bytes 27656 | tf_op jit(solution)/shard_map/ppermute | solution.py:33
  340.7 5.7 %collective-permute-start.16 = (bf16[18,1,256]{2,1,0:T(2,128)(2,1)S(1)}, bf16[18,1,256]{2,1,0:T(2,128)(2,1)S(1)}, u32[]{:S(2)}, u32[]{:S(2)}) collective-permute-start(bf16[18,1,256]{2,1,0:T(2,128)(2,1)S(1)} %get-tuple-element.63), channel_id=1, source_target_pairs={{0,1},{1,2},{2,3},{3,4},{4,5},{5,6},{6,7},{8,9},{9,10},{10,11},{11... | collective-permute-start | bytes 27656 | tf_op jit(solution)/shard_map/ppermute | solution.py:32
  346.6 1.3 copy-start.20
  346.7 1.3 copy-start.24
